TPU v7x, 32 devices: a whole 2x2x4 slice. The times are simulated.
32 devices in a mesh: blk: 8 (over z, x), grp: 4 (over y, core).
Axes of the slice: x: 2, y: 2, z: 4, core: 2. Of those that a mesh axis runs over, the one named last changes fastest.
Arguments:
- queries: bfloat16 [16384, 512], P(('blk', 'grp')), may hold values from -64 to 64
- keys: bfloat16 [16384, 128], P(('blk', 'grp')), may hold values from -8 to 8
- values: bfloat16 [16384, 128], P(('blk', 'grp')), may hold values from -6 to 6
- selected: int32 [32, 16], replicated, may hold values from 0 to 255, as said below
- key_in: bfloat16 [4096, 256], replicated, may hold values from -0.09375 to 0.09375
- key_out: bfloat16 [256, 128], replicated, may hold values from -0.375 to 0.375
- value_in: bfloat16 [4096, 256], replicated, may hold values from -0.09375 to 0.09375
- value_out: bfloat16 [256, 128], replicated, may hold values from -0.375 to 0.375
- positions: bfloat16 [2, 32, 128], replicated, may hold values from -5 to 5
- gate_weight: bfloat16 [512, 12], replicated, may hold values from -0.25 to 0.25
Outputs:
- attended: bfloat16 [16384, 512], P(('blk', 'grp'))
Inputs may be any that keep to these rules, and one draw needn't show every extreme that they name: `selected`: row d lists 16 different fine blocks. Write r = 32 and b = d // 4. Entry 0 is the first fine block of group d's own tokens. Every listed block j with j // r different from b has j // r < b, and no two listed blocks share a value of j // r other than b. Blocks with j // r == b may lie after group d's tokens.
All inputs are finite; a program needn't handle non-finite values.
Results may differ from a plain program's by a relative error of at most 0.004.
Values may be sent and summed in bfloat16 or wider, within the bound.
A program may use at most 64 MiB of HBM per device.

v0:
```python
import jax
import jax.numpy as jnp
from jax import lax
from jax.sharding import PartitionSpec as P

HEAD_DIM = 128
HEADS = 4
CMP_BLOCK = 32
SEL_BLOCK = 64
TOPN = 16
WINDOW = 512
NEG = -1e30


def from_behind(block, axis, distance):
    devices = range(lax.axis_size(axis))
    route = [(i - distance, i) for i in devices if i - distance in devices]
    return lax.ppermute(block, axis, route)


def compress(tokens, shift, w_in, w_out):
    count = tokens.shape[0] // CMP_BLOCK
    mixed = (
        tokens.astype(jnp.float32).reshape(count, CMP_BLOCK, HEAD_DIM)
        + shift.astype(jnp.float32)[None]
    )
    flat = mixed.astype(jnp.bfloat16).reshape(count, CMP_BLOCK * HEAD_DIM)
    hidden = jax.nn.silu(jnp.dot(flat, w_in, preferred_element_type=jnp.float32)).astype(
        jnp.bfloat16
    )
    return jnp.dot(hidden, w_out, preferred_element_type=jnp.float32).astype(jnp.bfloat16)


def attend(query_rows, query_pos, key_rows, value_rows, key_pos, span):
    scale = HEAD_DIM ** (-0.5)
    scores = (
        jnp.einsum("qhd,kd->qhk", query_rows, key_rows, preferred_element_type=jnp.float32) * scale
    )
    allowed = (
        (key_pos[None, :] <= query_pos[:, None])
        & (key_pos[None, :] > query_pos[:, None] - span)
        & (key_pos[None, :] >= 0)
    )
    scores = jnp.where(allowed[:, None, :], scores, NEG)
    top = jnp.max(scores, axis=2, keepdims=True)
    weights = jnp.exp(scores - top)
    total = jnp.sum(weights, axis=2)
    mixed = jnp.einsum(
        "qhk,kd->qhd", weights.astype(jnp.bfloat16), value_rows, preferred_element_type=jnp.float32
    )
    return mixed / total[..., None]


def make_fold(query_heads, query_pos):
    scale = HEAD_DIM ** (-0.5)
    toks = query_heads.shape[0]

    def fold(carry, piece, start):
        best, total, accum = carry
        piece_keys, piece_values = piece
        count = piece_keys.shape[0]
        key_end = jnp.arange(count, dtype=jnp.int32) * CMP_BLOCK + (CMP_BLOCK - 1)
        block_rows = toks
        while (
            block_rows > 32 and block_rows % 2 == 0 and (HEADS * block_rows * count * 4 > 1 << 24)
        ):
            block_rows = block_rows // 2
        steps = toks // block_rows

        def one(items):
            rows, pos, old_best, old_total, old_accum = items
            scores = (
                jnp.einsum("qhd,kd->qhk", rows, piece_keys, preferred_element_type=jnp.float32)
                * scale
            )
            scores = jnp.where((key_end[None, :] <= pos[:, None])[:, None, :], scores, NEG)
            new_best = jnp.maximum(old_best, jnp.max(scores, axis=2))
            weights = jnp.exp(scores - new_best[..., None])
            factor = jnp.exp(old_best - new_best)
            new_total = old_total * factor + jnp.sum(weights, axis=2)
            product = jnp.einsum(
                "qhk,kd->qhd",
                weights.astype(jnp.bfloat16),
                piece_values,
                preferred_element_type=jnp.float32,
            )
            return (new_best, new_total, old_accum * factor[..., None] + product)

        items = (
            query_heads.reshape(steps, block_rows, HEADS, HEAD_DIM),
            query_pos.reshape(steps, block_rows),
            best.reshape(steps, block_rows, HEADS),
            total.reshape(steps, block_rows, HEADS),
            accum.reshape(steps, block_rows, HEADS, HEAD_DIM),
        )
        new_best, new_total, new_accum = lax.map(one, items)
        return (
            new_best.reshape(toks, HEADS),
            new_total.reshape(toks, HEADS),
            new_accum.reshape(toks, HEADS, HEAD_DIM),
        )

    return fold


def per_device(
    queries, keys, values, selected, key_in, key_out, value_in, value_out, positions, gate_weight
):
    stretches = lax.axis_size("blk")
    group_size = lax.axis_size("grp")
    stretch = lax.axis_index("blk")
    column = lax.axis_index("grp")
    toks = queries.shape[0]
    seq_len = stretches * group_size * toks
    position = stretch * group_size + column
    query_pos = position * toks + jnp.arange(toks, dtype=jnp.int32)
    query_heads = queries.reshape(toks, HEADS, HEAD_DIM)
    row_keys, row_values = (
        lax.all_gather(keys, "grp", axis=0, tiled=True),
        lax.all_gather(values, "grp", axis=0, tiled=True),
    )
    fold = make_fold(query_heads, query_pos)
    start_state = (
        jnp.zeros((toks, HEADS), jnp.float32),
        jnp.ones((toks, HEADS), jnp.float32),
        jnp.zeros((toks, HEADS, HEAD_DIM), jnp.float32),
    )
    packed = (
        compress(row_keys, positions[0], key_in, key_out),
        compress(row_values, positions[1], value_in, value_out),
    )
    best, total, accum = fold(
        start_state,
        (
            lax.all_gather(packed[0], "blk", axis=0, tiled=True),
            lax.all_gather(packed[1], "blk", axis=0, tiled=True),
        ),
        jnp.int32(0),
    )
    coarse = accum / total[..., None]
    per_row = group_size * toks // SEL_BLOCK
    row_blocks = jnp.concatenate([row_keys, row_values], axis=1).reshape(
        per_row, SEL_BLOCK, 2 * HEAD_DIM
    )
    requests = jnp.take(selected.reshape(stretches, group_size, TOPN), column, axis=1)
    targets = jnp.arange(stretches, dtype=jnp.int32)
    match = (requests // per_row == stretch) & (targets[:, None] != stretch)
    picked = jnp.sum(jnp.where(match, requests % per_row, 0), axis=1)
    outgoing = jnp.take(row_blocks, picked, axis=0)
    incoming = lax.all_to_all(outgoing, "blk", split_axis=0, concat_axis=0, tiled=True)
    mine = lax.dynamic_index_in_dim(selected, position, 0, keepdims=False)
    owners = mine // per_row
    nearby = jnp.take(row_blocks, mine % per_row, axis=0)
    remote = jnp.take(incoming, owners, axis=0)
    fine_rows = jnp.where((owners == stretch)[:, None, None], nearby, remote).reshape(
        TOPN * SEL_BLOCK, 2 * HEAD_DIM
    )
    fine_keys = fine_rows[:, :HEAD_DIM]
    fine_values = fine_rows[:, HEAD_DIM:]
    fine_pos = (
        mine[:, None] * SEL_BLOCK + jnp.arange(SEL_BLOCK, dtype=jnp.int32)[None, :]
    ).reshape(-1)
    reach = (WINDOW + toks - 1) // toks
    moved_keys, moved_values = from_behind((keys, values), ("blk", "grp"), 1)
    key_parts = [moved_keys]
    value_parts = [moved_values]
    wide_keys = jnp.concatenate(key_parts + [keys], axis=0)
    wide_values = jnp.concatenate(value_parts + [values], axis=0)
    wide_pos = position * toks - reach * toks + jnp.arange((reach + 1) * toks, dtype=jnp.int32)
    block_rows = min(toks, 128)
    steps = toks // block_rows

    def both_blocks(index):
        first = index * block_rows
        rows = lax.dynamic_slice_in_dim(query_heads, first, block_rows, 0)
        pos = lax.dynamic_slice_in_dim(query_pos, first, block_rows, 0)
        fine_part = attend(rows, pos, fine_keys, fine_values, fine_pos, seq_len + 1)
        key_start = reach * toks + first - WINDOW
        near_keys = lax.dynamic_slice_in_dim(wide_keys, key_start, block_rows + WINDOW, 0)
        near_values = lax.dynamic_slice_in_dim(wide_values, key_start, block_rows + WINDOW, 0)
        near_pos = lax.dynamic_slice_in_dim(wide_pos, key_start, block_rows + WINDOW, 0)
        local_part = attend(rows, pos, near_keys, near_values, near_pos, WINDOW)
        return (fine_part, local_part)

    fine, local = lax.map(both_blocks, jnp.arange(steps, dtype=jnp.int32))
    fine = fine.reshape(toks, HEADS, HEAD_DIM)
    local = local.reshape(toks, HEADS, HEAD_DIM)
    gates = jax.nn.sigmoid(
        jnp.dot(queries, gate_weight, preferred_element_type=jnp.float32)
    ).reshape(toks, 3, HEADS)
    mixed = (
        gates[:, 0, :, None] * coarse + gates[:, 1, :, None] * fine + gates[:, 2, :, None] * local
    )
    return mixed.astype(jnp.bfloat16).reshape(toks, HEADS * HEAD_DIM)


def solution(mesh):
    return jax.shard_map(
        per_device,
        mesh=mesh,
        in_specs=(
            P(("blk", "grp"), None),
            P(("blk", "grp"), None),
            P(("blk", "grp"), None),
            P(),
            P(),
            P(),
            P(),
            P(),
            P(),
            P(),
        ),
        out_specs=P(("blk", "grp"), None),
        check_vma=False,
    )
```

profile of v0, /device:TPU:0, one launch (start us, length us, event | category | flops | bytes accessed | tf_op | source)
XLA Modules:
  0.0 162.3 jit_solution(4513411098601739997)
XLA Ops:
  0.0 3.2 %collective-permute-start = (bf16[512,128]{1,0:T(8,128)(2,1)}, bf16[512,128]{1,0:T(8,128)(2,1)}, u32[]{:S(2)}, u32[]{:S(2)}) collective-permute-start(bf16[512,128]{1,0:T(8,128)(2,1)} %param.13), channel_id=1, source_target_pairs={{0,1},{1,2},{2,3},{3,4},{4,5},{5,6},{6,7},{7,8},{8,9},{9,10},{10,1... | collective-permute-start | bytes 393224 | tf_op jit(solution)/shard_map/ppermute | solution.py:18
  3.2 4.5 %collective-permute-start.1 = (bf16[512,128]{1,0:T(8,128)(2,1)}, bf16[512,128]{1,0:T(8,128)(2,1)}, u32[]{:S(2)}, u32[]{:S(2)}) collective-permute-start(bf16[512,128]{1,0:T(8,128)(2,1)} %param.14), channel_id=1, source_target_pairs={{0,1},{1,2},{2,3},{3,4},{4,5},{5,6},{6,7},{7,8},{8,9},{9,10},{10,1... | collective-permute-start | bytes 393224 | tf_op jit(solution)/shard_map/ppermute | solution.py:18
  7.7 6.7 %all_gather.12 = bf16[2048,128]{1,0:T(8,128)(2,1)S(1)} all-gather(bf16[512,128]{1,0:T(8,128)(2,1)} %param.13), channel_id=1, replica_groups=mesh['blk'=8,'grp'=4] {'grp'}, dimensions={0}, use_global_device_ids=true | all-gather | bytes 655360 | tf_op jit(solution)/shard_map/all_gather | solution.py:119
  14.4 7.5 %all_gather.14 = bf16[2048,128]{1,0:T(8,128)(2,1)S(1)} all-gather(bf16[512,128]{1,0:T(8,128)(2,1)} %param.14), channel_id=1, replica_groups=mesh['blk'=8,'grp'=4] {'grp'}, dimensions={0}, use_global_device_ids=true | all-gather | bytes 655360 | tf_op jit(solution)/shard_map/all_gather | solution.py:120
  22.9 1.1 pad_maximum_fusion
  24.0 1.8 %gather_fusion.1 = bf16[8,64,256]{2,1,0:T(8,128)(2,1)S(1)} fusion(bf16[32,64,256]{2,1,0:T(8,128)(2,1)} %bitcast.141, s32[1024]{0:T(1024)S(1)} %pad_clamp_fusion.1), kind=kCustom, calls=%fused_computation.1 | custom fusion | bytes 524320 | tf_op jit(solution)/shard_map/jit(_take)/gather | solution.py:149
  26.6 6.0 %all-to-all-start = ((bf16[8,64,256]{2,1,0:T(8,128)(2,1)}), bf16[8,64,256]{2,1,0:T(8,128)(2,1)S(1)}, u32[]{:S(2)}, u32[]{:S(2)}) async-start(bf16[8,64,256]{2,1,0:T(8,128)(2,1)} %broadcast_select_fusion), calls=%async_computation | async-start | bytes 524288 | tf_op jit(solution)/shard_map/all_to_all | solution.py:150
  33.2 1.2 reshape.482
  34.4 1.2 reshape.485
  38.1 1.8 %convolution_convert_fusion.1 = bf16[64,128]{1,0:T(8,128)(2,1)S(1)} fusion(bf16[256,128]{1,0:T(8,128)(2,1)S(1)} %copy-done.9, bf16[4096,256]{1,0:T(8,128)(2,1)S(1)} %copy-done, f32[64,4096]{1,0:T(8,128)} %reshape.482, f32[4096]{0:T(1024)S(1)} %get-tuple-element.393), kind=kOutput, calls=%fused_computation.58 | convolution fusion | flops 139026432 | bytes 3244032 | tf_op jit(solution)/shard_map/dot_general | solution.py:31
  39.9 31.1 %all_gather.13 = bf16[512,128]{1,0:T(8,128)(2,1)S(1)} all-gather(bf16[64,128]{1,0:T(8,128)(2,1)S(1)} %convolution_convert_fusion.1), channel_id=1, replica_groups=mesh['blk'=8,'grp'=4] {'blk'}, dimensions={0}, use_global_device_ids=true | all-gather | bytes 147456 | tf_op jit(solution)/shard_map/all_gather | solution.py:135
  71.2 0.9 broadcast_compare_fusion.2
  73.0 0.9 fusion.30
  73.9 1.0 copy-done.1
  74.9 2.5 %convolution_convert_fusion = bf16[64,128]{1,0:T(8,128)(2,1)S(1)} fusion(bf16[256,128]{1,0:T(8,128)(2,1)S(1)} %copy-done.10, bf16[4096,256]{1,0:T(8,128)(2,1)} %param.18, f32[64,4096]{1,0:T(8,128)} %reshape.485, f32[4096]{0:T(1024)S(1)} %get-tuple-element.392), kind=kOutput, calls=%fused_computation.57 | convolution fusion | flops 139026432 | bytes 3244032 | tf_op jit(solution)/shard_map/dot_general | solution.py:31
  77.4 30.7 %all_gather.15 = bf16[512,128]{1,0:T(8,128)(2,1)S(1)} all-gather(bf16[64,128]{1,0:T(8,128)(2,1)S(1)} %convolution_convert_fusion), channel_id=1, replica_groups=mesh['blk'=8,'grp'=4] {'blk'}, dimensions={0}, use_global_device_ids=true | all-gather | bytes 147456 | tf_op jit(solution)/shard_map/all_gather | solution.py:136
  108.1 1.3 fusion.41
  109.5 4.3 %divide_multiply_fusion = f32[512,4,128]{0,2,1:T(8,128)} fusion(f32[512,512,4]{1,0,2:T(8,128)} %copy-done.1, f32[512,4]{0,1:T(4,128)S(1)} %broadcast_maximum_fusion, pred[512,512]{0,1:T(8,128)(4,1)S(1)} %broadcast_compare_fusion.2, f32[512,4]{0,1:T(4,128)S(1)} %get-tuple-element.395, f32[512,4]{0,1:T(4,128)S(1)} %get-tuple-element.394, ...), kind=kOutput, calls=%fused_computation.65 | convolution fusion | flops 273416192 | bytes 5668864 | tf_op jit(solution)/shard_map/while/body/eval_jaxpr/qhk,kd->qhd/dot_general | solution.py:81
  113.9 2.6 %copy.24 = f32[512,512]{1,0:T(8,128)} copy(f32[512,512]{0,1:T(8,128)} %bitcast.143) | data formatting | bytes 2097152 | tf_op jit(solution)/shard_map/mul | solution.py:192
  116.5 2.6 %gather_fusion = bf16[16,64,256]{2,1,0:T(8,128)(2,1)} fusion(bf16[32,64,256]{2,1,0:T(8,128)(2,1)} %bitcast.142, s32[1024]{0:T(1024)S(1)} %get-tuple-element.402), kind=kCustom, calls=%fused_computation | custom fusion | bytes 1048640 | tf_op jit(solution)/shard_map/jit(_take)/gather | solution.py:153
  121.4 0.9 pad_maximum_fusion.1
  122.3 1.6 %pad_maximum_fusion.2 = bf16[1024,128]{1,0:T(8,128)(2,1)} fusion(bf16[512,128]{1,0:T(8,128)(2,1)S(1)} %copy-done.6, bf16[512,128]{1,0:T(8,128)(2,1)} %collective-permute-done.1), kind=kLoop, calls=%fused_computation.77 | loop fusion | flops 524288 | bytes 524288 | tf_op jit(solution)/shard_map/concatenate | solution.py:168
  124.0 1.4 gather_fusion.2
  125.3 1.9 %fusion.49 = bf16[1024,256]{1,0:T(8,128)(2,1)S(1)} fusion(bf16[16,64,256]{2,1,0:T(8,128)(2,1)} %gather_fusion.2, bf16[16,64,256]{2,1,0:T(8,128)(2,1)} %gather_fusion, pred[1024]{0:T(1024)(128)(4,1)S(1)} %broadcast_in_dim.198, pred[1024]{0:T(1024)(128)(4,1)S(1)} %broadcast_in_dim.194, pred[1024]{0:T(1024)(128)(4,1)S(1)} %broadcast_in_dim.191), kind=kLoop, calls=%fused_computation.71 | loop fusion | flops 786432 | bytes 1575936 | tf_op jit(solution)/shard_map/jit(_where)/select_n | solution.py:155
  127.9 28.5 %while.24 = (s32[]{:T(128)}, f32[4,128,4,128]{3,2,1,0:T(4,128)}, f32[4,128,4,128]{3,2,1,0:T(4,128)}, s32[4]{0:T(128)S(1)}, s32[512]{0:T(512)}, /*index=5*/bf16[5...) while((s32[]{:T(128)}, f32[4,128,4,128]{3,2,1,0:T(4,128)}, ...), condition=%wide.region_8.9_spmd.clone, body=%wide.region_3.8_spmd.clone.sunk | while | flops 445252480 | bytes 15753344 | solution.py:185
  133.9 1.2 copy_dynamic-update-slice_fusion.3
  141.0 1.1 copy_dynamic-update-slice_fusion.3
  148.2 1.2 copy_dynamic-update-slice_fusion.3
  155.3 1.1 copy_dynamic-update-slice_fusion.3
  156.5 1.7 %mul.142 = f32[512,4,128]{2,1,0:T(4,128)S(1)} broadcast(f32[512,4]{1,0:T(8,128)} %copy.20), dimensions={0,1} | broadcast | bytes 1056768 | tf_op jit(solution)/shard_map/mul | solution.py:192
  158.2 1.6 mul.147
  159.7 2.5 %fusion.43 = bf16[512,512]{1,0:T(8,128)(2,1)} fusion(f32[64,8,4,128]{3,2,1,0:T(4,128)} %bitcast.145, f32[64,8,4,128]{3,2,1,0:T(4,128)S(1)} %bitcast.140, f32[512,512]{1,0:T(8,128)S(1)} %copy-done.2, f32[64,8,4,128]{3,2,1,0:T(4,128)S(1)} %bitcast.144, f32[64,8,4,128]{3,2,1,0:T(4,128)S(1)} %bitcast.139), kind=kLoop, calls=%fused_computation.61 | loop fusion | flops 1310720 | bytes 5767168 | tf_op jit(solution)/shard_map/convert_element_type | solution.py:194
  (150 shorter events, 29.8 us)
Async XLA Ops:
  0.0 38.1 %copy-start = (bf16[4096,256]{1,0:T(8,128)(2,1)S(1)}, bf16[4096,256]{1,0:T(8,128)(2,1)}, u32[]{:S(2)}) copy-start(bf16[4096,256]{1,0:T(8,128)(2,1)} %param.16) | copy-start | bytes 6291460
  0.0 121.4 %collective-permute-start = (bf16[512,128]{1,0:T(8,128)(2,1)}, bf16[512,128]{1,0:T(8,128)(2,1)}, u32[]{:S(2)}, u32[]{:S(2)}) collective-permute-start(bf16[512,128]{1,0:T(8,128)(2,1)} %param.13), channel_id=1, source_target_pairs={{0,1},{1,2},{2,3},{3,4},{4,5},{5,6},{6,7},{7,8},{8,9},{9,10},{10,1... | collective-permute-start | bytes 393224 | tf_op jit(solution)/shard_map/ppermute | solution.py:18
  3.2 119.1 %collective-permute-start.1 = (bf16[512,128]{1,0:T(8,128)(2,1)}, bf16[512,128]{1,0:T(8,128)(2,1)}, u32[]{:S(2)}, u32[]{:S(2)}) collective-permute-start(bf16[512,128]{1,0:T(8,128)(2,1)} %param.14), channel_id=1, source_target_pairs={{0,1},{1,2},{2,3},{3,4},{4,5},{5,6},{6,7},{7,8},{8,9},{9,10},{10,1... | collective-permute-start | bytes 393224 | tf_op jit(solution)/shard_map/ppermute | solution.py:18
  25.8 9.8 %copy-start.11 = (s32[32,16]{0,1:T(8,128)S(1)}, s32[32,16]{0,1:T(8,128)}, u32[]{:S(2)}) copy-start(s32[32,16]{0,1:T(8,128)} %param.15) | copy-start | bytes 6148
  25.8 12.3 %copy-start.12 = (bf16[2,32,128]{2,1,0:T(8,128)(2,1)S(1)}, bf16[2,32,128]{2,1,0:T(8,128)(2,1)}, u32[]{:S(2)}) copy-start(bf16[2,32,128]{2,1,0:T(8,128)(2,1)} %param.20) | copy-start | bytes 49156
  25.8 12.3 %copy-start.9 = (bf16[256,128]{1,0:T(8,128)(2,1)S(1)}, bf16[256,128]{1,0:T(8,128)(2,1)}, u32[]{:S(2)}) copy-start(bf16[256,128]{1,0:T(8,128)(2,1)} %param.17) | copy-start | bytes 196612
  26.6 97.4 %all-to-all-start = ((bf16[8,64,256]{2,1,0:T(8,128)(2,1)}), bf16[8,64,256]{2,1,0:T(8,128)(2,1)S(1)}, u32[]{:S(2)}, u32[]{:S(2)}) async-start(bf16[8,64,256]{2,1,0:T(8,128)(2,1)} %broadcast_select_fusion), calls=%async_computation | async-start | bytes 524288 | tf_op jit(solution)/shard_map/all_to_all | solution.py:150
  35.6 35.4 %copy-start.3 = (bf16[512,512]{1,0:T(8,128)(2,1)S(1)}, bf16[512,512]{1,0:T(8,128)(2,1)}, u32[]{:S(2)}) copy-start(bf16[512,512]{1,0:T(8,128)(2,1)} %param.12) | copy-start | bytes 1572868
  73.0 1.9 %copy-start.1 = (f32[512,512,4]{1,0,2:T(8,128)}, f32[512,512,4]{1,0,2:T(8,128)S(1)}, u32[]{:S(2)}) copy-start(f32[512,512,4]{1,0,2:T(8,128)S(1)} %get-tuple-element.400) | copy-start | bytes 12582916
  73.0 1.9 %copy-start.10 = (bf16[256,128]{1,0:T(8,128)(2,1)S(1)}, bf16[256,128]{1,0:T(8,128)(2,1)}, u32[]{:S(2)}) copy-start(bf16[256,128]{1,0:T(8,128)(2,1)} %param.19) | copy-start | bytes 196612
  74.9 33.2 %copy-start.13 = (bf16[512,12]{0,1:T(8,128)(2,1)S(1)}, bf16[512,12]{0,1:T(8,128)(2,1)}, u32[]{:S(2)}) copy-start(bf16[512,12]{0,1:T(8,128)(2,1)} %param.21) | copy-start | bytes 36868
  74.9 34.6 %copy-start.19 = (s32[16]{0:T(128)S(1)}, s32[16]{0:T(128)}, u32[]{:S(2)}) copy-start(s32[16]{0:T(128)} %get-tuple-element.380) | copy-start | bytes 196
  109.5 4.4 %copy-start.17 = (s32[16]{0:T(128)S(1)}, s32[16]{0:T(128)}, u32[]{:S(2)}) copy-start(s32[16]{0:T(128)} %get-tuple-element.397) | copy-start | bytes 196
  109.5 4.4 %copy-start.18 = (s32[16]{0:T(128)S(1)}, s32[16]{0:T(128)}, u32[]{:S(2)}) copy-start(s32[16]{0:T(128)} %get-tuple-element.398) | copy-start | bytes 196
  113.9 5.4 %copy-start.16 = (pred[16]{0:T(512)(128)(4,1)S(1)}, pred[16]{0:T(512)(128)(4,1)}, u32[]{:S(2)}) copy-start(pred[16]{0:T(512)(128)(4,1)} %get-tuple-element.379) | copy-start | bytes 52
  113.9 5.6 %copy-start.15 = (pred[16]{0:T(512)(128)(4,1)S(1)}, pred[16]{0:T(512)(128)(4,1)}, u32[]{:S(2)}) copy-start(pred[16]{0:T(512)(128)(4,1)} %get-tuple-element.396) | copy-start | bytes 52
  113.9 7.5 %copy-start.5 = (bf16[512,128]{1,0:T(8,128)(2,1)S(1)}, bf16[512,128]{1,0:T(8,128)(2,1)}, u32[]{:S(2)}) copy-start(bf16[512,128]{1,0:T(8,128)(2,1)} %param.13) | copy-start | bytes 393220
  113.9 8.4 %copy-start.6 = (bf16[512,128]{1,0:T(8,128)(2,1)S(1)}, bf16[512,128]{1,0:T(8,128)(2,1)}, u32[]{:S(2)}) copy-start(bf16[512,128]{1,0:T(8,128)(2,1)} %param.14) | copy-start | bytes 393220
  122.3 5.6 %copy-start.14 = (s32[16]{0:T(128)S(1)}, s32[16]{0:T(128)}, u32[]{:S(2)}) copy-start(s32[16]{0:T(128)} %broadcast_multiply_fusion) | copy-start | bytes 196
  130.4 1.2 copy-start.8
  132.3 1.1 copy-start.7
  137.5 1.2 copy-start.8
  139.5 1.1 copy-start.7
  144.7 1.2 copy-start.8
  146.6 1.1 copy-start.7
  151.8 1.2 copy-start.8
  153.7 1.1 copy-start.7
  156.5 3.3 %copy-start.2 = (f32[512,512]{1,0:T(8,128)S(1)}, f32[512,512]{1,0:T(8,128)}, u32[]{:S(2)}) copy-start(f32[512,512]{1,0:T(8,128)} %copy.24) | copy-start | bytes 3145732
  156.5 3.3 %copy-start.4 = (f32[4,128,4,128]{3,2,1,0:T(4,128)S(1)}, f32[4,128,4,128]{3,2,1,0:T(4,128)}, u32[]{:S(2)}) copy-start(f32[4,128,4,128]{3,2,1,0:T(4,128)} %get-tuple-element.299) | copy-start | bytes 3145732
where the time goes:
time: 163 us; the launch traced here: 162 us
  blocking collectives  76 us (47%)
  local copies, waits for them, and re-layouts  26.9 us (17%)
  other arithmetic  22.7 us (14%)
  matrix products  19.6 us (12%)
  starting transfers between devices  13.7 us (8%)
  loops' own time  3.12 us (2%)
    all_gather x1, blocking collectives, per_device(): lax.all_gather(packed[0], 'blk', axis=0, tiled=True)  31.1 us
    all_gather x1, blocking collectives, per_device(): lax.all_gather(packed[1], 'blk', axis=0, tiled=True)  30.7 us
    ppermute x2, starting transfers between devices, from_behind(): return lax.ppermute(block, axis, route)  7.7 us
    all_gather x1, blocking collectives, per_device(): lax.all_gather(values, 'grp', axis=0, tiled=True)  7.48 us
    all_gather x1, blocking collectives, per_device(): lax.all_gather(keys, 'grp', axis=0, tiled=True)  6.7 us
    all_to_all x1, starting transfers between devices, per_device(): lax.all_to_all(outgoing, 'blk', split_axis=0, concat_axis=0, tiled=True)  6 us
    dynamic_update_slice x4, local copies, waits for them, and re-layouts, per_device(): fine, local = lax.map(both_blocks, jnp.arange(steps, dtype=jnp.int32))  4.64 us
    dot_general x8, matrix products, attend(): jnp.einsum('qhd,kd->qhk', query_rows, key_rows, preferred_element_type=jn...  4.55 us
  transfers between devices with their start and end apart: 3, of which 0 were waited for; matrix products, arithmetic and copies ran while one was open for 20% of the time, Pallas kernels for 0%

commit v1 on v0

--- a/solution.py
+++ b/solution.py
@@ -10,6 +10,11 @@
 TOPN = 16
 WINDOW = 512
 NEG = -1e30
+
+
+def all_by_exchange(array, axis, dim):
+    outgoing = jnp.stack([array] * lax.axis_size(axis))
+    return jnp.concatenate(lax.all_to_all(outgoing, axis, 0, 0), axis=dim)
 
 
 def from_behind(block, axis, distance):
@@ -133,7 +138,7 @@
         start_state,
         (
             lax.all_gather(packed[0], "blk", axis=0, tiled=True),
-            lax.all_gather(packed[1], "blk", axis=0, tiled=True),
+            all_by_exchange(packed[1], "blk", 0),
         ),
         jnp.int32(0),
     )

time: 163 us -> 145 us (0.89)
  blocking collectives: 76 us -> 49.3 us
  local copies, waits for them, and re-layouts: 26.9 us -> 32.4 us
  starting transfers between devices: 13.7 us -> 16.5 us
    all_gather x1 -> x0, blocking collectives: 30.7 us -> none  [per_device(): lax.all_gather(packed[1], 'blk', axis=0, tiled=True)]
    all_to_all x0 -> x1, starting transfers between devices: none -> 6.15 us  [all_by_exchange(): return jnp.concatenate(lax.all_to_all(outgoing, axis, 0, 0), axis=dim)]
    sub x8, other arithmetic: 2.99 us -> 0.33 us  [attend(): query_pos[:, None] - span]
    ppermute x2, starting transfers between devices: 7.7 us -> 5.8 us  [from_behind(): return lax.ppermute(block, axis, route)]
    all_gather x1, blocking collectives: 7.48 us -> 9.11 us  [per_device(): lax.all_gather(values, 'grp', axis=0, tiled=True)]
  transfers between devices with their start and end apart: 3 -> 4, of which waited for: 0 -> 1; matrix products, arithmetic and copies ran while one was open for 20% -> 28% of each run, Pallas kernels for 0% -> 0%
where the time goes in v1:
time: 145 us; the launch traced here: 144 us
  blocking collectives  49.3 us (34%)
  local copies, waits for them, and re-layouts  32.4 us (22%)
  other arithmetic  23 us (16%)
  matrix products  18.6 us (13%)
  starting transfers between devices  16.5 us (11%)
  loops' own time  2.87 us (2%)
    all_gather x1, blocking collectives, per_device(): lax.all_gather(packed[0], 'blk', axis=0, tiled=True)  31.9 us
    all_gather x1, blocking collectives, per_device(): lax.all_gather(values, 'grp', axis=0, tiled=True)  9.11 us
    all_gather x1, blocking collectives, per_device(): lax.all_gather(keys, 'grp', axis=0, tiled=True)  8.24 us
    all_to_all x1, starting transfers between devices, all_by_exchange(): return jnp.concatenate(lax.all_to_all(outgoing, axis, 0, 0), axis=dim)  6.15 us
    ppermute x2, starting transfers between devices, from_behind(): return lax.ppermute(block, axis, route)  5.8 us
    dynamic_update_slice x4, local copies, waits for them, and re-layouts, per_device(): fine, local = lax.map(both_blocks, jnp.arange(steps, dtype=jnp.int32))  4.59 us
    all_to_all x1, starting transfers between devices, per_device(): lax.all_to_all(outgoing, 'blk', split_axis=0, concat_axis=0, tiled=True)  4.55 us
    dot_general x8, matrix products, attend(): jnp.einsum('qhd,kd->qhk', query_rows, key_rows, preferred_element_type=jn...  4.55 us
  transfers between devices with their start and end apart: 4, of which 1 were waited for; matrix products, arithmetic and copies ran while one was open for 28% of the time, Pallas kernels for 0%

profile of v1, /device:TPU:0, one launch (start us, length us, event | category | flops | bytes accessed | tf_op | source)
XLA Modules:
  0.0 144.2 jit_solution(11631161596228009814)
XLA Ops:
  0.0 3.2 %collective-permute-start.1 = (bf16[512,128]{1,0:T(8,128)(2,1)}, bf16[512,128]{1,0:T(8,128)(2,1)}, u32[]{:S(2)}, u32[]{:S(2)}) collective-permute-start(bf16[512,128]{1,0:T(8,128)(2,1)} %param.14), channel_id=1, source_target_pairs={{0,1},{1,2},{2,3},{3,4},{4,5},{5,6},{6,7},{7,8},{8,9},{9,10},{10,1... | collective-permute-start | bytes 393224 | tf_op jit(solution)/shard_map/ppermute | solution.py:23
  3.2 9.1 %all_gather.11 = bf16[2048,128]{1,0:T(8,128)(2,1)S(1)} all-gather(bf16[512,128]{1,0:T(8,128)(2,1)} %param.14), channel_id=1, replica_groups=mesh['blk'=8,'grp'=4] {'grp'}, dimensions={0}, use_global_device_ids=true | all-gather | bytes 655360 | tf_op jit(solution)/shard_map/all_gather | solution.py:125
  13.0 1.2 reshape.491
  14.2 1.8 %convolution_convert_fusion = bf16[64,128]{1,0:T(8,128)(2,1)S(1)} fusion(bf16[256,128]{1,0:T(8,128)(2,1)S(1)} %copy-done.10, bf16[4096,256]{1,0:T(8,128)(2,1)S(1)} %copy-done, f32[64,4096]{1,0:T(8,128)} %reshape.491, f32[4096]{0:T(1024)S(1)} %get-tuple-element.393), kind=kOutput, calls=%fused_computation.57 | convolution fusion | flops 139026432 | bytes 3244032 | tf_op jit(solution)/shard_map/dot_general | solution.py:36
  16.7 6.2 %all-to-all-start = ((bf16[8,64,128]{2,1,0:T(8,128)(2,1)}), bf16[8,64,128]{2,1,0:T(8,128)(2,1)S(1)}, u32[]{:S(2)}, u32[]{:S(2)}) async-start(bf16[8,64,128]{2,1,0:T(8,128)(2,1)} %stack.2), calls=%async_computation | async-start | bytes 262144 | tf_op jit(solution)/shard_map/all_to_all | solution.py:17
  22.8 2.6 %collective-permute-start = (bf16[512,128]{1,0:T(8,128)(2,1)S(1)}, bf16[512,128]{1,0:T(8,128)(2,1)}, u32[]{:S(2)}, u32[]{:S(2)}) collective-permute-start(bf16[512,128]{1,0:T(8,128)(2,1)S(1)} %copy-done.6), channel_id=1, source_target_pairs={{0,1},{1,2},{2,3},{3,4},{4,5},{5,6},{6,7},{7,8},{8,9},{9,10},{10,1... | collective-permute-start | bytes 393224 | tf_op jit(solution)/shard_map/ppermute | solution.py:23
  25.5 8.2 %all_gather.9 = bf16[2048,128]{1,0:T(8,128)(2,1)S(1)} all-gather(bf16[512,128]{1,0:T(8,128)(2,1)S(1)} %copy-done.6), channel_id=1, replica_groups=mesh['blk'=8,'grp'=4] {'grp'}, dimensions={0}, use_global_device_ids=true | all-gather | bytes 655360 | tf_op jit(solution)/shard_map/all_gather | solution.py:124
  33.7 1.2 reshape.488
  34.9 1.1 pad_maximum_fusion
  39.3 2.5 %convolution_convert_fusion.1 = bf16[64,128]{1,0:T(8,128)(2,1)S(1)} fusion(bf16[256,128]{1,0:T(8,128)(2,1)S(1)} %copy-done.11, bf16[4096,256]{1,0:T(8,128)(2,1)} %param.16, f32[64,4096]{1,0:T(8,128)} %reshape.488, f32[4096]{0:T(1024)S(1)} %get-tuple-element.392), kind=kOutput, calls=%fused_computation.58 | convolution fusion | flops 139026432 | bytes 3244032 | tf_op jit(solution)/shard_map/dot_general | solution.py:36
  41.8 31.9 %all_gather.10 = bf16[512,128]{1,0:T(8,128)(2,1)S(1)} all-gather(bf16[64,128]{1,0:T(8,128)(2,1)S(1)} %convolution_convert_fusion.1), channel_id=1, replica_groups=mesh['blk'=8,'grp'=4] {'blk'}, dimensions={0}, use_global_device_ids=true | all-gather | bytes 147456 | tf_op jit(solution)/shard_map/all_gather | solution.py:140
  79.1 1.8 %gather_fusion.1 = bf16[8,64,256]{2,1,0:T(8,128)(2,1)S(1)} fusion(bf16[32,64,256]{2,1,0:T(8,128)(2,1)} %bitcast.142, s32[1024]{0:T(1024)S(1)} %pad_clamp_fusion.1), kind=kCustom, calls=%fused_computation.1 | custom fusion | bytes 524320 | tf_op jit(solution)/shard_map/jit(_take)/gather | solution.py:154
  80.9 1.4 broadcast_select_fusion
  82.3 1.3 pad_clamp_fusion
  83.6 2.6 %gather_fusion = bf16[16,64,256]{2,1,0:T(8,128)(2,1)} fusion(bf16[32,64,256]{2,1,0:T(8,128)(2,1)} %bitcast.143, s32[1024]{0:T(1024)S(1)} %get-tuple-element.402), kind=kCustom, calls=%fused_computation | custom fusion | bytes 1048640 | tf_op jit(solution)/shard_map/jit(_take)/gather | solution.py:158
  90.3 1.6 %copy.22 = f32[512,4]{1,0:T(8,128)} copy(f32[512,4]{0,1:T(4,128)} %get-tuple-element.389) | data formatting | bytes 16384 | tf_op jit(solution)/shard_map/mul | solution.py:197
  91.9 1.6 %copy.27 = f32[512,4]{1,0:T(8,128)} copy(f32[512,4]{0,1:T(4,128)} %get-tuple-element.390) | data formatting | bytes 16384 | tf_op jit(solution)/shard_map/mul | solution.py:197
  94.5 1.6 %pad_maximum_fusion.2 = bf16[1024,128]{1,0:T(8,128)(2,1)} fusion(bf16[512,128]{1,0:T(8,128)(2,1)S(1)} %copy-done.7, bf16[512,128]{1,0:T(8,128)(2,1)} %collective-permute-done.1), kind=kLoop, calls=%fused_computation.77 | loop fusion | flops 524288 | bytes 524288 | tf_op jit(solution)/shard_map/concatenate | solution.py:173
  96.1 4.6 %all-to-all-start.1 = ((bf16[8,64,256]{2,1,0:T(8,128)(2,1)}), bf16[8,64,256]{2,1,0:T(8,128)(2,1)S(1)}, u32[]{:S(2)}, u32[]{:S(2)}) async-start(bf16[8,64,256]{2,1,0:T(8,128)(2,1)} %broadcast_select_fusion), calls=%async_computation.1 | async-start | bytes 524288 | tf_op jit(solution)/shard_map/all_to_all | solution.py:155
  100.6 4.4 %divide_multiply_fusion = f32[512,4,128]{0,2,1:T(8,128)} fusion(bf16[512,128,1]{1,0,2:T(8,128)(2,1)S(1)} %bitcast.147, f32[512,512,4]{1,0,2:T(8,128)} %copy-done.1, f32[512,4]{0,1:T(4,128)S(1)} %broadcast_maximum_fusion, pred[512,512]{0,1:T(8,128)(4,1)S(1)} %broadcast_compare_fusion.2, f32[512,4]{0,1:T(4,128)} %get-tuple-element.395, ...), kind=kOutput, calls=%fused_computation.65 | convolution fusion | flops 273416192 | bytes 5668864 | tf_op jit(solution)/shard_map/while/body/eval_jaxpr/qhk,kd->qhd/dot_general | solution.py:86
  105.0 2.5 %copy.26 = f32[512,512]{1,0:T(8,128)} copy(f32[512,512]{0,1:T(8,128)} %bitcast.144) | data formatting | bytes 2097152 | tf_op jit(solution)/shard_map/mul | solution.py:197
  107.5 1.3 all-to-all-done.1
  108.9 1.5 %gather_fusion.2 = bf16[16,64,256]{2,1,0:T(8,128)(2,1)} fusion(bf16[8,64,256]{2,1,0:T(8,128)(2,1)S(1)} %all-to-all-done.1, s32[1024]{0:T(1024)} %get-tuple-element.401), kind=kCustom, calls=%fused_computation.2 | custom fusion | bytes 1048640 | tf_op jit(solution)/shard_map/jit(_take)/gather | solution.py:159
  110.4 1.9 %fusion.49 = bf16[1024,256]{1,0:T(8,128)(2,1)S(1)} fusion(bf16[16,64,256]{2,1,0:T(8,128)(2,1)} %gather_fusion.2, bf16[16,64,256]{2,1,0:T(8,128)(2,1)} %gather_fusion, pred[1024]{0:T(1024)(128)(4,1)S(1)} %copy-done.15, pred[1024]{0:T(1024)(128)(4,1)S(1)} %copy-done.17, pred[1024]{0:T(1024)(128)(4,1)S(1)} %copy-done.16), kind=kLoop, calls=%fused_computation.71 | loop fusion | flops 786432 | bytes 1575936 | tf_op jit(solution)/shard_map/jit(_where)/select_n | solution.py:160
  113.0 25.4 %while.24 = (s32[]{:T(128)}, f32[4,128,4,128]{3,2,1,0:T(4,128)}, f32[4,128,4,128]{3,2,1,0:T(4,128)}, s32[4]{0:T(128)S(1)}, s32[512]{0:T(512)S(1)}, /*index=5*/bf...) while((s32[]{:T(128)}, f32[4,128,4,128]{3,2,1,0:T(4,128)}, ...), condition=%wide.region_8.9_spmd.clone, body=%wide.region_3.8_spmd.clone.sunk | while | flops 445252480 | bytes 15753344 | solution.py:190
  118.2 1.1 copy_dynamic-update-slice_fusion.3
  124.5 1.1 copy_dynamic-update-slice_fusion.3
  130.9 1.1 copy_dynamic-update-slice_fusion.3
  137.2 1.2 copy_dynamic-update-slice_fusion.3
  138.4 1.7 %mul.142 = f32[512,4,128]{2,1,0:T(4,128)S(1)} broadcast(f32[512,4]{1,0:T(8,128)} %copy.22), dimensions={0,1} | broadcast | bytes 1056768 | tf_op jit(solution)/shard_map/mul | solution.py:197
  140.1 1.6 %mul.147 = f32[512,4,128]{2,1,0:T(4,128)S(1)} broadcast(f32[512,4]{1,0:T(8,128)} %copy.27), dimensions={0,1} | broadcast | bytes 1056768 | tf_op jit(solution)/shard_map/mul | solution.py:197
  141.7 2.5 %fusion.43 = bf16[512,512]{1,0:T(8,128)(2,1)} fusion(f32[64,8,4,128]{3,2,1,0:T(4,128)} %bitcast.146, f32[64,8,4,128]{3,2,1,0:T(4,128)S(1)} %bitcast.141, f32[512,512]{1,0:T(8,128)S(1)} %copy-done.2, f32[64,8,4,128]{3,2,1,0:T(4,128)S(1)} %bitcast.145, f32[64,8,4,128]{3,2,1,0:T(4,128)S(1)} %bitcast.140), kind=kLoop, calls=%fused_computation.61 | loop fusion | flops 1310720 | bytes 5767168 | tf_op jit(solution)/shard_map/convert_element_type | solution.py:199
  (152 shorter events, 33.8 us)
Async XLA Ops:
  0.0 14.2 %copy-start = (bf16[4096,256]{1,0:T(8,128)(2,1)S(1)}, bf16[4096,256]{1,0:T(8,128)(2,1)}, u32[]{:S(2)}) copy-start(bf16[4096,256]{1,0:T(8,128)(2,1)} %param.18) | copy-start | bytes 6291460
  0.0 14.2 %copy-start.10 = (bf16[256,128]{1,0:T(8,128)(2,1)S(1)}, bf16[256,128]{1,0:T(8,128)(2,1)}, u32[]{:S(2)}) copy-start(bf16[256,128]{1,0:T(8,128)(2,1)} %param.19) | copy-start | bytes 196612
  0.0 94.4 %collective-permute-start.1 = (bf16[512,128]{1,0:T(8,128)(2,1)}, bf16[512,128]{1,0:T(8,128)(2,1)}, u32[]{:S(2)}, u32[]{:S(2)}) collective-permute-start(bf16[512,128]{1,0:T(8,128)(2,1)} %param.14), channel_id=1, source_target_pairs={{0,1},{1,2},{2,3},{3,4},{4,5},{5,6},{6,7},{7,8},{8,9},{9,10},{10,1... | collective-permute-start | bytes 393224 | tf_op jit(solution)/shard_map/ppermute | solution.py:23
  14.2 8.6 %copy-start.6 = (bf16[512,128]{1,0:T(8,128)(2,1)S(1)}, bf16[512,128]{1,0:T(8,128)(2,1)}, u32[]{:S(2)}) copy-start(bf16[512,128]{1,0:T(8,128)(2,1)} %param.13) | copy-start | bytes 393220
  16.7 79.4 %all-to-all-start = ((bf16[8,64,128]{2,1,0:T(8,128)(2,1)}), bf16[8,64,128]{2,1,0:T(8,128)(2,1)S(1)}, u32[]{:S(2)}, u32[]{:S(2)}) async-start(bf16[8,64,128]{2,1,0:T(8,128)(2,1)} %stack.2), calls=%async_computation | async-start | bytes 262144 | tf_op jit(solution)/shard_map/all_to_all | solution.py:17
  22.8 70.7 %collective-permute-start = (bf16[512,128]{1,0:T(8,128)(2,1)S(1)}, bf16[512,128]{1,0:T(8,128)(2,1)}, u32[]{:S(2)}, u32[]{:S(2)}) collective-permute-start(bf16[512,128]{1,0:T(8,128)(2,1)S(1)} %copy-done.6), channel_id=1, source_target_pairs={{0,1},{1,2},{2,3},{3,4},{4,5},{5,6},{6,7},{7,8},{8,9},{9,10},{10,1... | collective-permute-start | bytes 393224 | tf_op jit(solution)/shard_map/ppermute | solution.py:23
  25.5 10.6 %copy-start.12 = (s32[32,16]{0,1:T(8,128)S(1)}, s32[32,16]{0,1:T(8,128)}, u32[]{:S(2)}) copy-start(s32[32,16]{0,1:T(8,128)} %param.15) | copy-start | bytes 6148
  25.5 13.8 %copy-start.11 = (bf16[256,128]{1,0:T(8,128)(2,1)S(1)}, bf16[256,128]{1,0:T(8,128)(2,1)}, u32[]{:S(2)}) copy-start(bf16[256,128]{1,0:T(8,128)(2,1)} %param.17) | copy-start | bytes 196612
  36.0 37.7 %copy-start.3 = (bf16[512,512]{1,0:T(8,128)(2,1)S(1)}, bf16[512,512]{1,0:T(8,128)(2,1)}, u32[]{:S(2)}) copy-start(bf16[512,512]{1,0:T(8,128)(2,1)} %param.12) | copy-start | bytes 1572868
  75.0 2.0 %copy-start.1 = (f32[512,512,4]{1,0,2:T(8,128)}, f32[512,512,4]{1,0,2:T(8,128)S(1)}, u32[]{:S(2)}) copy-start(f32[512,512,4]{1,0,2:T(8,128)S(1)} %get-tuple-element.400) | copy-start | bytes 12582916
  75.0 2.6 %copy-start.4 = (bf16[512,512]{1,0:T(8,128)(2,1)S(1)}, bf16[512,512]{1,0:T(8,128)(2,1)}, u32[]{:S(2)}) copy-start(bf16[512,512]{1,0:T(8,128)(2,1)} %param.12) | copy-start | bytes 1572868
  75.1 2.6 %copy-start.13 = (bf16[512,12]{0,1:T(8,128)(2,1)S(1)}, bf16[512,12]{0,1:T(8,128)(2,1)}, u32[]{:S(2)}) copy-start(bf16[512,12]{0,1:T(8,128)(2,1)} %param.21) | copy-start | bytes 36868
  75.1 3.4 %copy-start.18 = (s32[8]{0:T(128)S(1)}, s32[8]{0:T(128)}, u32[]{:S(2)}) copy-start(s32[8]{0:T(128)} %fusion.63) | copy-start | bytes 100
  75.1 3.4 %copy-start.19 = (s32[16]{0:T(128)S(1)}, s32[16]{0:T(128)}, u32[]{:S(2)}) copy-start(s32[16]{0:T(128)} %get-tuple-element.380) | copy-start | bytes 196
  77.0 17.5 %copy-start.7 = (bf16[512,128]{1,0:T(8,128)(2,1)S(1)}, bf16[512,128]{1,0:T(8,128)(2,1)}, u32[]{:S(2)}) copy-start(bf16[512,128]{1,0:T(8,128)(2,1)} %param.14) | copy-start | bytes 393220
  96.1 12.8 %all-to-all-start.1 = ((bf16[8,64,256]{2,1,0:T(8,128)(2,1)}), bf16[8,64,256]{2,1,0:T(8,128)(2,1)S(1)}, u32[]{:S(2)}, u32[]{:S(2)}) async-start(bf16[8,64,256]{2,1,0:T(8,128)(2,1)} %broadcast_select_fusion), calls=%async_computation.1 | async-start | bytes 524288 | tf_op jit(solution)/shard_map/all_to_all | solution.py:155
  105.0 5.4 %copy-start.15 = (pred[1024]{0:T(1024)(128)(4,1)S(1)}, pred[1024]{0:T(1024)(128)(4,1)}, u32[]{:S(2)}) copy-start(pred[1024]{0:T(1024)(128)(4,1)} %broadcast_in_dim.198) | copy-start | bytes 3076
  105.0 5.4 %copy-start.16 = (pred[1024]{0:T(1024)(128)(4,1)S(1)}, pred[1024]{0:T(1024)(128)(4,1)}, u32[]{:S(2)}) copy-start(pred[1024]{0:T(1024)(128)(4,1)} %broadcast_in_dim.191) | copy-start | bytes 3076
  105.0 5.4 %copy-start.17 = (pred[1024]{0:T(1024)(128)(4,1)S(1)}, pred[1024]{0:T(1024)(128)(4,1)}, u32[]{:S(2)}) copy-start(pred[1024]{0:T(1024)(128)(4,1)} %broadcast_in_dim.194) | copy-start | bytes 3076
  107.5 5.5 %copy-start.14 = (s32[16]{0:T(128)S(1)}, s32[16]{0:T(128)}, u32[]{:S(2)}) copy-start(s32[16]{0:T(128)} %broadcast_multiply_fusion) | copy-start | bytes 196
  114.7 1.2 copy-start.9
  116.6 1.1 copy-start.8
  121.1 1.2 copy-start.9
  123.0 1.1 copy-start.8
  127.4 1.2 copy-start.9
  129.3 1.1 copy-start.8
  133.7 1.2 copy-start.9
  135.7 1.1 copy-start.8
  138.4 3.3 %copy-start.2 = (f32[512,512]{1,0:T(8,128)S(1)}, f32[512,512]{1,0:T(8,128)}, u32[]{:S(2)}) copy-start(f32[512,512]{1,0:T(8,128)} %copy.26) | copy-start | bytes 3145732
  138.4 3.3 %copy-start.5 = (f32[4,128,4,128]{3,2,1,0:T(4,128)S(1)}, f32[4,128,4,128]{3,2,1,0:T(4,128)}, u32[]{:S(2)}) copy-start(f32[4,128,4,128]{3,2,1,0:T(4,128)} %get-tuple-element.299) | copy-start | bytes 3145732
